TPU v7x, 128 devices: a whole 4x4x4 slice. The times are simulated.
128 devices in a mesh: seq: 32 (over z, y, core), tp: 4 (over x).
Axes of the slice: x: 4, y: 4, z: 4, core: 2. Of those that a mesh axis runs over, the one named last changes fastest.
Arguments:
- tokens: bfloat16 [65536, 2048], P('seq'), may hold values from -36 to 36
- gain: bfloat16 [2048], replicated, may hold values from 0.099609375 to 1.8984375
- w_in: bfloat16 [2048, 16, 160], P(None, 'tp'), may hold values from -0.125 to 0.125
- conv_taps: bfloat16 [3, 16, 160], P(None, 'tp'), may hold values from -2.5 to 2.5
- w_out: bfloat16 [2048, 2048], P(None, 'tp'), may hold values from -0.125 to 0.125
Outputs:
- result: bfloat16 [65536, 2048], P('seq', 'tp')
All inputs are finite; a program needn't handle non-finite values.
Results may differ from a plain program's by a relative error of at most 0.014.
Values may be sent and summed in bfloat16 or wider, within the bound.
A program may use at most 128 MiB of HBM per device.

v0:
```python
import math

import jax
import jax.numpy as jnp
from jax import lax
from jax.sharding import PartitionSpec as P

DK = 16
DV = 128


epsilon = 1e-06


def from_behind(block, axis, distance):
    devices = range(lax.axis_size(axis))
    route = [(i - distance, i) for i in devices if i - distance in devices]
    return lax.ppermute(block, axis, route)


def carried_in(x, axis, combine, identity):
    size, position = (lax.axis_size(axis), lax.axis_index(axis))
    everything = jax.tree.map(
        lambda part, kind: lax.all_gather(part.astype(kind), axis),
        x,
        (jnp.bfloat16, jnp.bfloat16, jnp.bfloat16),
    )
    start = jax.tree.map(
        lambda part, zero: jnp.broadcast_to(jnp.asarray(zero, part.dtype), part.shape), x, identity
    )

    def lap(k, before):
        reached = k < position
        new = combine(
            before, jax.tree.map(lambda part, own: part[k].astype(own.dtype), everything, x)
        )
        return jax.tree.map(lambda a, b: jnp.where(reached, a, b), new, before)

    return lax.fori_loop(0, size, lap, start)


def taylor_terms(mixed):
    queries = mixed[..., :DK]
    key_rows = mixed[..., DK : 2 * DK]
    value_rows = mixed[..., 2 * DK :]
    factor = 1.0 / math.sqrt(DK)
    query_float = queries.astype(jnp.float32)
    key_float = key_rows.astype(jnp.float32)
    query_lin = (query_float * factor).astype(jnp.bfloat16)
    outer_query = query_float[..., :, None] * query_float[..., None, :] * (0.5 * factor * factor)
    query_sq = outer_query.reshape(outer_query.shape[:-2] + (DK * DK,)).astype(jnp.bfloat16)
    outer_key = key_float[..., :, None] * key_float[..., None, :]
    key_sq = outer_key.reshape(outer_key.shape[:-2] + (DK * DK,)).astype(jnp.bfloat16)
    return (queries, key_rows, value_rows, query_lin, query_sq, key_sq)


def body(tokens, gain, w_in, conv_taps, w_out):
    length = tokens.shape[0]
    factor = 1.0 / math.sqrt(DK)
    row_float = tokens.astype(jnp.float32)
    mean_square = jnp.mean(row_float * row_float, axis=-1, keepdims=True)
    normed = (row_float * lax.rsqrt(mean_square + epsilon) * gain.astype(jnp.float32)).astype(
        jnp.bfloat16
    )
    projected = jnp.einsum("td,dhc->htc", normed, w_in, preferred_element_type=jnp.float32).astype(
        jnp.bfloat16
    )
    before = from_behind(projected[:, -2:], "seq", 1)
    padded = jnp.concatenate([before, projected], 1)
    tap_float = conv_taps.astype(jnp.float32)[:, :, None, :]
    mixed = (
        padded[:, :-2] * tap_float[0]
        + padded[:, 1:-1] * tap_float[1]
        + padded[:, 2:] * tap_float[2]
    ).astype(jnp.bfloat16)
    queries, key_rows, value_rows, query_lin, query_sq, key_sq = taylor_terms(mixed)
    state_sum = jnp.sum(value_rows.astype(jnp.float32), 1)
    linear_state = jnp.einsum(
        "gzu,gzw->guw", key_rows, value_rows, preferred_element_type=jnp.float32
    )
    state_sq = jnp.einsum("htf,htv->hfv", key_sq, value_rows, preferred_element_type=jnp.float32)

    def combine(earlier_part, later_part):
        return tuple((first + second for first, second in zip(earlier_part, later_part)))

    identity = (jnp.zeros_like(state_sum), jnp.zeros_like(linear_state), jnp.zeros_like(state_sq))
    prefix = carried_in((state_sum, linear_state, state_sq), "seq", combine, identity)
    prefix_sum, prefix_lin, prefix_sq = tuple((member.astype(jnp.bfloat16) for member in prefix))
    causal = jnp.arange(length)[:, None] >= jnp.arange(length)[None, :]

    def head_output(operands):
        query_head, key_head, value_head, lin_head, square_head, low_sum, low_lin, low_sq = operands
        scores = jnp.dot(query_head, key_head.T, preferred_element_type=jnp.float32) * factor
        weights = jnp.where(causal, 1.0 + scores + 0.5 * scores * scores, 0.0).astype(jnp.bfloat16)
        numerator = jnp.dot(weights, value_head, preferred_element_type=jnp.float32)
        numerator = numerator + low_sum.astype(jnp.float32)[None, :]
        numerator = numerator + jnp.dot(lin_head, low_lin, preferred_element_type=jnp.float32)
        numerator = numerator + jnp.dot(square_head, low_sq, preferred_element_type=jnp.float32)
        spread = jnp.mean(numerator * numerator, axis=-1, keepdims=True)
        return (numerator * lax.rsqrt(spread + epsilon)).astype(jnp.bfloat16)

    outputs = lax.map(
        head_output,
        (queries, key_rows, value_rows, query_lin, query_sq, prefix_sum, prefix_lin, prefix_sq),
    )
    weight_three = w_out.reshape(-1, DV, w_out.shape[1])
    summed_out = jnp.einsum(
        "htv,hvd->td",
        lax.all_gather(outputs, "tp", axis=0, tiled=True),
        weight_three,
        preferred_element_type=jnp.float32,
    )
    return summed_out.astype(jnp.bfloat16)


def solution(mesh):
    return jax.shard_map(
        body,
        mesh=mesh,
        in_specs=(P("seq", None), P(), P(None, "tp", None), P(None, "tp", None), P(None, "tp")),
        out_specs=P("seq", "tp"),
        check_vma=False,
    )
```

profile of v0, /device:TPU:1, one launch (start us, length us, event | category | flops | bytes accessed | tf_op | source)
XLA Modules:
  0.0 309.5 jit_solution(5859051998875324483)
XLA Ops:
  7.4 5.5 %fusion.37 = f32[2048]{0:T(1024)S(1)} fusion(bf16[2048,2048]{1,0:T(8,128)(2,1)} %param.9), kind=kLoop, calls=%fused_computation.43 | loop fusion | flops 12580864 | bytes 8396800 | tf_op jit(solution)/shard_map/reduce_sum | solution.py:61
  13.1 5.9 %fusion.40 = f32[2048,640]{0,1:S(1)} fusion(bf16[2048,640]{0,1:T(8,128)(2,1)S(1)} %bitcast.91, bf16[2048,2048]{1,0:T(8,128)(2,1)S(1)} %copy-done.2, f32[2048]{0:T(1024)S(1)} %convert_element_type.119, f32[2048]{0:T(1024)S(1)} %add_rsqrt_fusion.1), kind=kOutput, calls=%fused_computation.46 | convolution fusion | flops 5385486336 | bytes 16269312
  19.6 4.6 %collective-permute-start = (bf16[4,2,160]{1,2,0:T(8,128)(2,1)S(1)}, bf16[4,2,160]{1,2,0:T(8,128)(2,1)S(1)}, u32[]{:S(2)}, u32[]{:S(2)}) collective-permute-start(bf16[4,2,160]{1,2,0:T(8,128)(2,1)S(1)} %slice.39), channel_id=1, source_target_pairs={{0,4},{4,8},{8,12},{12,16},{16,20},{20,24},{24,28},{28,32},{32,36}... | collective-permute-start | bytes 7688 | tf_op jit(solution)/shard_map/ppermute | solution.py:18
  24.2 2.2 collective-permute-done
  26.4 3.3 %add_convert_fusion = bf16[4,2048,160]{1,2,0:T(8,128)(2,1)S(1)} fusion(bf16[4,2048,160]{1,2,0:T(8,128)(2,1)S(1)} %convert_bitcast_fusion, bf16[4,2,160]{1,2,0:T(8,128)(2,1)S(1)} %collective-permute-done, f32[4,160]{1,0:T(4,128)S(1)} %get-tuple-element.411, f32[4,160]{1,0:T(4,128)S(1)} %get-tuple-element.412, f32[4,160]{1,0:T(4,128)S(1)} %get-tuple-element.410), kind=kLoop, calls=%fused_computation.51 | loop fusion | flops 19660800 | bytes 5253120 | tf_op jit(solution)/shard_map/convert_element_type | solution.py:75
  30.8 3.1 %multiply_convert_fusion.1 = (bf16[4,2048,16,16]{1,3,2,0:T(8,128)(2,1)}, bf16[4,2048,16,16]{1,3,2,0:T(8,128)(2,1)S(1)}) fusion(f32[4,2048,16]{1,2,0:T(8,128)S(1)} %get-tuple-element.404, f32[4,2048,16]{1,2,0:T(8,128)S(1)} %get-tuple-element.405), kind=kLoop, calls=%fused_computation.47 | loop fusion | flops 10485760 | bytes 9437184 | tf_op jit(solution)/shard_map/convert_element_type | solution.py:51
  33.9 1.9 convolution_convert_fusion
  36.0 3.2 %slice_reduce_fusion = (bf16[4,128]{1,0:T(4,128)(2,1)S(1)}, bf16[4,2048,128]{1,2,0:T(8,128)(2,1)}) fusion(bf16[4,2048,160]{1,2,0:T(8,128)(2,1)} %copy-done.1), kind=kLoop, calls=%fused_computation.70 | loop fusion | flops 1048064 | bytes 4195328 | tf_op jit(solution)/shard_map/reduce_sum | solution.py:77
  39.2 28.3 %all-gather.3 = bf16[32,4,128]{2,1,0:T(4,128)(2,1)S(1)} all-gather(bf16[1,4,128]{2,1,0:T(4,128)(2,1)S(1)} %bitcast.97), channel_id=2, replica_groups=mesh['seq'=32,'tp'=4] {'seq'}, dimensions={0}, use_global_device_ids=true | all-gather | bytes 33792 | tf_op jit(solution)/shard_map/all_gather | solution.py:24
  67.5 2.3 convolution_convert_fusion.1
  69.8 25.3 %all-gather.1 = bf16[128,16,128]{2,1,0:T(8,128)(2,1)} all-gather(bf16[4,16,128]{2,1,0:T(8,128)(2,1)S(1)} %convolution_convert_fusion.1), channel_id=3, replica_groups=mesh['seq'=32,'tp'=4] {'seq'}, dimensions={0}, use_global_device_ids=true | all-gather | bytes 540672 | tf_op jit(solution)/shard_map/all_gather | solution.py:24
  95.1 1.7 multiply_convert_fusion.3
  96.8 64.0 %while.32 = (s32[]{:T(128)}, f32[4,128]{1,0:T(4,128)S(1)}, f32[4,16,128]{2,1,0:T(8,128)S(1)}, f32[4,256,128]{2,1,0:T(8,128)S(1)}, s32[]{:T(128)}, /*index=5*/bf1...) while((s32[]{:T(128)}, f32[4,128]{1,0:T(4,128)S(1)}, ...), condition=%wide.region_3.4_spmd.clone, body=%wide.region_2.3_spmd.clone.sunk | while | flops 559108 | bytes 1397905 | solution.py:39
  97.6 1.2 add_select_fusion.8
  99.6 1.2 add_select_fusion.8
  101.6 1.2 add_select_fusion.8
  103.6 1.2 add_select_fusion.8
  105.6 1.2 add_select_fusion.8
  107.6 1.2 add_select_fusion.8
  109.6 1.2 add_select_fusion.8
  111.6 1.2 add_select_fusion.8
  113.6 1.2 add_select_fusion.8
  115.6 1.2 add_select_fusion.8
  117.6 1.2 add_select_fusion.8
  119.6 1.2 add_select_fusion.8
  121.6 1.2 add_select_fusion.8
  123.6 1.2 add_select_fusion.8
  127.6 1.2 add_select_fusion.8
  143.6 1.2 add_select_fusion.8
  160.9 51.5 %while.31 = (s32[]{:T(128)}, bf16[4,2048,128]{2,1,0:T(8,128)(2,1)}, bf16[4,2048,16]{1,2,0:T(8,128)(2,1)}, bf16[4,2048,16]{1,2,0:T(8,128)(2,1)}, bf16[4,2048,128]...) while((s32[]{:T(128)}, bf16[4,2048,128]{2,1,0:T(8,128)(2,1)}, ...), condition=%wide.region_6.7_spmd.clone, body=%wide.region_4.6_spmd.clone.sunk | while | flops 1385957504 | bytes 10789757 | solution.py:102
  160.9 6.7 %fusion.68 = f32[2048,128]{0,1:T(8,128)} fusion(f32[128]{0:T(128)S(1)} %fusion.67, bf16[4,2048,128]{1,2,0:T(8,128)(2,1)} %get-tuple-element.585, s32[]{:T(128)S(6)} %copy.46, bf16[4,2048,16]{1,2,0:T(8,128)(2,1)} %get-tuple-element.584, bf16[4,2048,16]{1,2,0:T(8,128)(2,1)} %get-tuple-element.583), kind=kOutput, calls=%fused_computation.7.clone.1 | convolution fusion | flops 1241776128 | bytes 1705984 | tf_op jit(solution)/shard_map/while/body/eval_jaxpr/dot_general | solution.py:95
  167.6 1.6 fusion.66
  169.2 1.6 multiply_reduce_fusion.2
  172.0 1.9 constant_dynamic-update-slice_fusion.2
  173.8 6.6 %fusion.68 = f32[2048,128]{0,1:T(8,128)} fusion(f32[128]{0:T(128)S(1)} %fusion.67, bf16[4,2048,128]{1,2,0:T(8,128)(2,1)} %get-tuple-element.585, s32[]{:T(128)S(6)} %copy.46, bf16[4,2048,16]{1,2,0:T(8,128)(2,1)} %get-tuple-element.584, bf16[4,2048,16]{1,2,0:T(8,128)(2,1)} %get-tuple-element.583), kind=kOutput, calls=%fused_computation.7.clone.1 | convolution fusion | flops 1241776128 | bytes 1705984 | tf_op jit(solution)/shard_map/while/body/eval_jaxpr/dot_general | solution.py:95
  180.5 1.6 fusion.66
  182.1 1.6 multiply_reduce_fusion.2
  184.8 1.9 constant_dynamic-update-slice_fusion.2
  186.7 6.6 %fusion.68 = f32[2048,128]{0,1:T(8,128)} fusion(f32[128]{0:T(128)S(1)} %fusion.67, bf16[4,2048,128]{1,2,0:T(8,128)(2,1)} %get-tuple-element.585, s32[]{:T(128)S(6)} %copy.46, bf16[4,2048,16]{1,2,0:T(8,128)(2,1)} %get-tuple-element.584, bf16[4,2048,16]{1,2,0:T(8,128)(2,1)} %get-tuple-element.583), kind=kOutput, calls=%fused_computation.7.clone.1 | convolution fusion | flops 1241776128 | bytes 1705984 | tf_op jit(solution)/shard_map/while/body/eval_jaxpr/dot_general | solution.py:95
  193.4 1.6 fusion.66
  194.9 1.6 multiply_reduce_fusion.2
  197.7 1.9 constant_dynamic-update-slice_fusion.2
  199.6 6.6 %fusion.68 = f32[2048,128]{0,1:T(8,128)} fusion(f32[128]{0:T(128)S(1)} %fusion.67, bf16[4,2048,128]{1,2,0:T(8,128)(2,1)} %get-tuple-element.585, s32[]{:T(128)S(6)} %copy.46, bf16[4,2048,16]{1,2,0:T(8,128)(2,1)} %get-tuple-element.584, bf16[4,2048,16]{1,2,0:T(8,128)(2,1)} %get-tuple-element.583), kind=kOutput, calls=%fused_computation.7.clone.1 | convolution fusion | flops 1241776128 | bytes 1705984 | tf_op jit(solution)/shard_map/while/body/eval_jaxpr/dot_general | solution.py:95
  206.2 1.6 fusion.66
  207.8 1.6 multiply_reduce_fusion.2
  210.6 1.9 constant_dynamic-update-slice_fusion.2
  212.5 81.7 %all-gather.7.cloned.1.call-done = bf16[16,2048,128]{2,1,0:T(8,128)(2,1)} async-done(((bf16[4,2048,128]{2,1,0:T(8,128)(2,1)}), bf16[16,2048,128]{2,1,0:T(8,128)(2,1)}) %all-gather.7.cloned.1.call-update) | async-done | bytes 8388624 | tf_op jit(solution)/shard_map/all_gather | solution.py:109
  294.2 8.5 %bitcast_convert_fusion = bf16[2048,512]{1,0:T(8,128)(2,1)} fusion(bf16[16,2048,128]{2,1,0:T(8,128)(2,1)} %all-gather.7.cloned.1.call-done, bf16[16,128,512]{2,1,0:T(8,128)(2,1)} %bitcast.98), kind=kOutput, calls=%fused_computation.52 | convolution fusion | flops 4296015872 | bytes 12582912 | tf_op jit(solution)/shard_map/htv,hvd->td/dot_general | solution.py:107
  (123 shorter events, 50.8 us)
Async XLA Ops:
  6.5 6.3 %copy-start = (bf16[2048,4,160]{0,2,1:T(8,128)(2,1)S(1)}, bf16[2048,4,160]{0,2,1:T(8,128)(2,1)}, u32[]{:S(2)}) copy-start(bf16[2048,4,160]{0,2,1:T(8,128)(2,1)} %param.11) | copy-start | bytes 7864324
  6.5 90.3 %all-gather.9.cloned.1.call-start = ((), (), s32[]{:S(2)}) async-start(), calls=%async_computation.1 | async-start | bytes 8650752 | tf_op jit(solution)/shard_map/all_gather | solution.py:24
  6.5 6.6 %copy-start.2 = (bf16[2048,2048]{1,0:T(8,128)(2,1)S(1)}, bf16[2048,2048]{1,0:T(8,128)(2,1)}, u32[]{:S(2)}) copy-start(bf16[2048,2048]{1,0:T(8,128)(2,1)} %param.9) | copy-start | bytes 25165828
  19.0 5.2 %copy-start.3 = (bf16[3,4,160]{2,1,0:T(4,128)(2,1)S(1)}, bf16[3,4,160]{2,1,0:T(4,128)(2,1)}, u32[]{:S(2)}) copy-start(bf16[3,4,160]{2,1,0:T(4,128)(2,1)} %param.12) | copy-start | bytes 11524
  19.6 6.8 %collective-permute-start = (bf16[4,2,160]{1,2,0:T(8,128)(2,1)S(1)}, bf16[4,2,160]{1,2,0:T(8,128)(2,1)S(1)}, u32[]{:S(2)}, u32[]{:S(2)}) collective-permute-start(bf16[4,2,160]{1,2,0:T(8,128)(2,1)S(1)} %slice.39), channel_id=1, source_target_pairs={{0,4},{4,8},{8,12},{12,16},{16,20},{20,24},{24,28},{28,32},{32,36}... | collective-permute-start | bytes 7688 | tf_op jit(solution)/shard_map/ppermute | solution.py:18
  29.7 4.2 %copy-start.1 = (bf16[4,2048,160]{1,2,0:T(8,128)(2,1)}, bf16[4,2048,160]{1,2,0:T(8,128)(2,1)S(1)}, u32[]{:S(2)}) copy-start(bf16[4,2048,160]{1,2,0:T(8,128)(2,1)S(1)} %add_convert_fusion) | copy-start | bytes 7864324
  35.9 258.3 %all-gather.7.cloned.1.call-start = ((), (), s32[]{:S(2)}) async-start(), calls=%async_computation | async-start | bytes 10485760 | tf_op jit(solution)/shard_map/all_gather | solution.py:109
Sparse Core Ops, SparseCore 0:
  36.0 57.6 all-gather.8
  212.6 81.5 all-gather.6
where the time goes:
time: 313 us; the launch traced here: 310 us
  waiting for transfers between devices  83.9 us (27%)
  other arithmetic  82.7 us (26%)
  matrix products  58.1 us (19%)
  blocking collectives  53.7 us (17%)
  between operations  13.6 us (4%)
  local copies, waits for them, and re-layouts  11.9 us (4%)
  starting transfers between devices  4.64 us (1%)
    all_gather x1, waiting for transfers between devices, body(): lax.all_gather(outputs, 'tp', axis=0, tiled=True)  81.7 us
    select_n x96, other arithmetic, lap(): return jax.tree.map(lambda a, b: jnp.where(reached, a, b), new, before)  63.2 us
    all_gather x2, blocking collectives, carried_in(): lax.all_gather(part.astype(kind), axis)  53.7 us
    dot_general x4, matrix products, head_output(): numerator = jnp.dot(weights, value_head, preferred_element_type=jnp.float32)  26.6 us
    dynamic_update_slice x8, local copies, waits for them, and re-layouts, body(): lax.map(head_output, (queries, key_rows, value_rows, query_lin, query_sq,...  11.6 us
    dot_general x1, matrix products, body(): jnp.einsum('htv,hvd->td', lax.all_gather(outputs, 'tp', axis=0, tiled=Tru...  8.5 us
    dot_general x4, matrix products, head_output(): jnp.dot(lin_head, low_lin, preferred_element_type=jnp.float32)  6.58 us
    dot_general x4, matrix products, head_output(): jnp.dot(square_head, low_sq, preferred_element_type=jnp.float32)  6.3 us
  transfers between devices with their start and end apart: 3, of which 2 were waited for; matrix products, arithmetic and copies ran while one was open for 2% of the time, Pallas kernels for 0%

commit v1 on v0

v1 whole, which is shorter than its diff:
```python
import functools
import math

import jax
import jax.numpy as jnp
import numpy as np
from jax import lax
from jax.experimental import pallas as pl
from jax.experimental.pallas import tpu as pltpu
from jax.sharding import PartitionSpec as P

DK = 16
DV = 128
HL = 4
T = 2048
D = 2048
C = 256
NC = T // C
F = 160
FP = 256
VW = HL * DV
QW = HL * 2 * DK
SEQ = 32
TP = 4
CHIPS = SEQ // 2
ROWS = HL * F // CHIPS
EPS = 1e-06
MESH = pl.DeviceIdType.MESH
F32 = jnp.float32
BF16 = jnp.bfloat16


def feature_maps():
    eq = np.zeros((2, FP, HL * FP), np.float32)
    ek = np.zeros((2, HL * F, FP), np.float32)
    one = QW
    for h in range(HL):
        q0, k0 = 2 * DK * h, 2 * DK * h + DK
        f = 0
        for i in range(DK):
            for j in range(i, DK):
                eq[0, q0 + i, h * FP + f] = (1.0 if i == j else 2.0) / 32.0
                eq[1, q0 + j, h * FP + f] = 1.0
                ek[0, h * F + f, k0 + i] = 1.0
                ek[1, h * F + f, k0 + j] = 1.0
                f += 1
        for i in range(DK):
            eq[0, q0 + i, h * FP + f] = 0.25
            eq[1, one, h * FP + f] = 1.0
            ek[0, h * F + f, k0 + i] = 1.0
            ek[1, h * F + f, one] = 1.0
            f += 1
        eq[0, one, h * FP + f] = 1.0
        eq[1, one, h * FP + f] = 1.0
        ek[0, h * F + f, one] = 1.0
        ek[1, h * F + f, one] = 1.0
    return eq.astype(jnp.bfloat16), ek.astype(jnp.bfloat16)


def kernel(
    x_hbm, gain_ref, wt_hbm, taps_ref, wo_hbm, eq_hbm, ek_hbm,
    out_ref,
    xv, wv, eqv, ekv, taps, pf, vb, qk, kt, sc, nl, pq, sb, r1, p2, r2, pp, wf, ho, g, ob,
    in_sem, x_sem, wo_sem, halo_s, halo_r, s1_s, s1_r, s2_s, s2_r, s3_s, s3_r,
    wx_s, wx_r, wa_s, wa_r, wb_s, wb_r, wc_s, wc_r, a_s, a_r, b_s, b_r, own_s,
):
    s = lax.axis_index("seq")
    t = lax.axis_index("tp")
    chip = s // 2
    core = s % 2
    zc = s // 8
    yc = (s // 2) % 4
    sib = s + 1 - 2 * core

    def remote(src, dst, ss, rs, dev):
        return pltpu.make_async_remote_copy(
            src_ref=src, dst_ref=dst, send_sem=ss, recv_sem=rs, device_id=dev, device_id_type=MESH
        )

    def xpeer(d):
        return (s, lax.rem(t + d, TP))

    def ypeer(d):
        return (zc * 8 + lax.rem(yc + d, 4) * 2 + core, t)

    def zpeer(d):
        return (lax.rem(zc + d, 4) * 8 + yc * 2 + core, t)

    wcopy = pltpu.make_async_copy(wt_hbm, wv, in_sem.at[0])
    wcopy.start()
    order = [NC - 1] + list(range(NC - 1))
    xcopies = {}
    for c in order:
        xcopies[c] = pltpu.make_async_copy(x_hbm.at[pl.ds(c * C, C)], xv.at[pl.ds(c * C, C)], x_sem.at[c])
        xcopies[c].start()
    ekcopy = pltpu.make_async_copy(ek_hbm, ekv, in_sem.at[1])
    ekcopy.start()
    eqcopy = pltpu.make_async_copy(eq_hbm, eqv, in_sem.at[2])
    eqcopy.start()
    wocopies = [
        pltpu.make_async_copy(
            wo_hbm.at[zz, yy, cc], wf.at[0, zz, yy, cc], wo_sem
        )
        for zz in range(0) for yy in range(0) for cc in range(0)
    ]
    wocopy = pltpu.make_async_copy(wo_hbm, wf.at[0], wo_sem)
    wocopy.start()

    barrier = pltpu.get_barrier_semaphore()

    def greet(j, carry):
        pl.semaphore_signal(barrier, inc=1, device_id=(lax.rem(s + j, SEQ), t), device_id_type=MESH)
        return carry

    lax.fori_loop(1, SEQ, greet, 0)
    for d in range(1, TP):
        pl.semaphore_signal(barrier, inc=1, device_id=xpeer(d), device_id_type=MESH)

    row = lax.broadcasted_iota(jnp.int32, (160, 128), 0)
    col = lax.broadcasted_iota(jnp.int32, (160, 128), 1)
    pick_v = (row == col + 2 * DK).astype(F32).astype(BF16)
    for k in range(3):
        tk = taps_ref[k]
        tv = jnp.dot(tk, pick_v, preferred_element_type=F32)
        tq = jnp.zeros((1, QW), F32)
        for h in range(HL):
            taps[k : k + 1, h * DV : (h + 1) * DV] = tv[h : h + 1, :]
            pick_q = ((row + 2 * DK * h == col) & (row < 2 * DK)).astype(F32).astype(BF16)
            tq = tq + jnp.dot(tk, pick_q, preferred_element_type=F32)[h : h + 1, :]
        taps[k : k + 1, VW:] = tq

    wcopy.wait()
    gain = gain_ref[...].astype(F32)
    wg = wv
    for r in range(0, HL * 160, 32):
        wg[r : r + 32, :] = (wv[r : r + 32, :].astype(F32) * gain).astype(BF16)

    def project(c):
        xt = xv[c * C : (c + 1) * C, :]
        xf = xt.astype(F32)
        scale = lax.rsqrt(jnp.mean(xf * xf, axis=-1, keepdims=True) + EPS)
        pr = lax.dot_general(xt, wg[...], (((1,), (1,)), ((), ())), preferred_element_type=F32)
        pr = (pr * scale).astype(BF16).astype(F32)
        base = 8 + c * C
        for h in range(HL):
            pf[base : base + C, h * DV : (h + 1) * DV] = pr[:, h * 160 + 32 : h * 160 + 160]
            pf[base : base + C, VW + 32 * h : VW + 32 * h + 32] = pr[:, h * 160 : h * 160 + 32]

    xcopies[NC - 1].wait()
    project(NC - 1)

    pl.semaphore_wait(barrier, SEQ - 1 + TP - 1)
    halo = remote(
        pf.at[pl.ds(T, 8)], pf.at[pl.ds(0, 8)], halo_s, halo_r, (lax.rem(s + 1, SEQ), t)
    )
    halo.start()
    wx = []
    for d in range(1, TP):
        cp = remote(
            wo_hbm.at[zc, yc, core], wf.at[TP - d, zc, yc, core], wx_s.at[d - 1], wx_r.at[d - 1], xpeer(d)
        )
        cp.start()
        wx.append(cp)

    def states(c):
        ext = pf[c * C : c * C + C + 8, :]
        mixed = (
            ext[6 : 6 + C] * taps[0:1, :] + ext[7 : 7 + C] * taps[1:2, :] + ext[8 : 8 + C] * taps[2:3, :]
        )
        vb[c * C : (c + 1) * C, :] = mixed[:, :VW].astype(BF16)
        qkb = mixed[:, VW:].astype(BF16)
        qk[c * C : (c + 1) * C, :] = qkb
        qt = jnp.transpose(qkb.astype(F32)).astype(BF16)
        kt[c] = qt
        qe = jnp.concatenate([qt, jnp.ones((FP - QW, C), BF16)], axis=0)
        fk = (
            jnp.dot(ekv[0], qe, preferred_element_type=F32) * jnp.dot(ekv[1], qe, preferred_element_type=F32)
        ).astype(BF16)
        for h in range(HL):
            sc[c, h * F : (h + 1) * F, :] = jnp.dot(
                fk[h * F : (h + 1) * F, :], vb[c * C : (c + 1) * C, h * DV : (h + 1) * DV],
                preferred_element_type=F32,
            )

    ekcopy.wait()
    for c in range(NC - 1):
        xcopies[c].wait()
        project(c)
        if c >= 1:
            states(c)
    states(NC - 1)

    for cp in wx:
        cp.wait()
    wa = []
    for d in range(1, 4):
        src = wf.at[1:4, zc, yc, core, :, 0:256]
        cp = remote(src, src, wa_s.at[d - 1], wa_r.at[d - 1], ypeer(d))
        cp.start()
        wa.append(cp)
        src = wf.at[1:4, zc, yc, core, :, 256:512]
        cp = remote(src, src, wa_s.at[d + 2], wa_r.at[d + 2], zpeer(d))
        cp.start()
        wa.append(cp)

    halo.wait()
    pf[0:8, :] = jnp.where(s == 0, 0.0, pf[0:8, :])
    states(0)

    run = jnp.zeros((HL * F, DV), F32)
    for c in range(NC):
        part = sc[c]
        sc[c] = run
        run = run + part
    for k in range(CHIPS):
        sb[k] = run[k * ROWS : (k + 1) * ROWS, :].astype(BF16)

    def spread(i, carry):
        k = lax.rem(chip + i, CHIPS)
        remote(sb.at[k], r1.at[s], s1_s, s1_r, (2 * k, t)).start()
        return carry

    lax.fori_loop(1, CHIPS, spread, 0)

    @pl.when(core == 1)
    def _():
        cp = remote(sb.at[chip], r1.at[s], s3_s, s1_r, (s - 1, t))
        cp.start()
        cp.wait_send()

    @pl.when(core == 0)
    def _():
        r1[s] = sb[chip]

    eqcopy.wait()
    pos = lax.broadcasted_iota(jnp.int32, (C, C), 0) >= lax.broadcasted_iota(jnp.int32, (C, C), 1)

    def local(c):
        q = qk[c * C : (c + 1) * C, :]
        qe = jnp.concatenate([q, jnp.ones((C, FP - QW), BF16)], axis=1)
        ktc = (kt[c].astype(F32) * 0.25).astype(BF16)
        for h in range(HL):
            fq = (
                jnp.dot(qe, eqv[0, :, h * FP : (h + 1) * FP], preferred_element_type=F32)
                * jnp.dot(qe, eqv[1, :, h * FP : (h + 1) * FP], preferred_element_type=F32)
            ).astype(BF16)
            pq[c * C : (c + 1) * C, h * FP : (h + 1) * FP] = fq
            parts = []
            if h > 0:
                parts.append(jnp.zeros((32 * h, C), BF16))
            parts.append(ktc[32 * h + 16 : 32 * h + 32, :])
            parts.append(jnp.zeros((QW - 32 * h - 16, C), BF16))
            keys = jnp.concatenate(parts, axis=0)
            up = jnp.dot(q, keys, preferred_element_type=F32) + 1.0
            w = jnp.where(pos, up * up * 0.5 + 0.5, 0.0).astype(BF16)
            num = jnp.dot(w, vb[c * C : (c + 1) * C, h * DV : (h + 1) * DV], preferred_element_type=F32)
            if c > 0:
                before = jnp.concatenate(
                    [sc[c, h * F : (h + 1) * F, :].astype(BF16), jnp.zeros((FP - F, DV), BF16)], axis=0
                )
                num = num + jnp.dot(fq, before, preferred_element_type=F32)
            nl[c * C : (c + 1) * C, h * DV : (h + 1) * DV] = num

    for c in range(NC // 2):
        local(c)

    @pl.when(core == 0)
    def _():
        pltpu.make_async_copy(r1.at[0 : SEQ - 1], r1.at[0 : SEQ - 1], s1_r).wait()
        acc = jnp.zeros((ROWS, DV), F32)
        for k in range(SEQ):
            p2[k // 2, k % 2] = acc.astype(BF16)
            acc = acc + r1[k].astype(F32)
        r2[chip] = p2[chip]

        def back(i, carry):
            k = lax.rem(chip + i, CHIPS)
            remote(p2.at[k], r2.at[chip], s2_s, s2_r, (2 * k, t)).start()
            return carry

        lax.fori_loop(1, CHIPS, back, 0)

    pltpu.make_async_copy(sb.at[0 : CHIPS - 1], sb.at[0 : CHIPS - 1], s1_s).wait()
    for c in range(NC // 2, NC):
        local(c)

    for cp in wa:
        cp.wait()
    wb = []
    for d in range(1, 4):
        src = wf.at[1:4, zc, :, core, :, 0:256]
        cp = remote(src, src, wb_s.at[d - 1], wb_r.at[d - 1], zpeer(d))
        cp.start()
        wb.append(cp)
        src = wf.at[1:4, :, yc, core, :, 256:512]
        cp = remote(src, src, wb_s.at[d + 2], wb_r.at[d + 2], ypeer(d))
        cp.start()
        wb.append(cp)

    fwd = remote(r2, r2, s3_s, s3_r, (sib, t))

    @pl.when(core == 0)
    def _():
        pltpu.make_async_copy(p2.at[0 : CHIPS - 1], p2.at[0 : CHIPS - 1], s2_s).wait()
        pltpu.make_async_copy(r2.at[0 : CHIPS - 1], r2.at[0 : CHIPS - 1], s2_r).wait()
        fwd.start()

    @pl.when(core == 1)
    def _():
        fwd.wait_recv()

    pp[...] = jnp.zeros_like(pp)
    for k in range(CHIPS):
        h, o = k // 4, (k % 4) * ROWS
        pp[h, o : o + ROWS, :] = r2[k, core]

    def finish(i, dst):
        base = pl.multiple_of(i * C, C)
        for h in range(HL):
            num = nl[pl.ds(base, C), h * DV : (h + 1) * DV] + jnp.dot(
                pq[pl.ds(base, C), h * FP : (h + 1) * FP], pp[h], preferred_element_type=F32
            )
            spread_ = jnp.mean(num * num, axis=-1, keepdims=True)
            dst[:, h * DV : (h + 1) * DV] = (num * lax.rsqrt(spread_ + EPS)).astype(BF16)

    sent = {}
    for half in range(2):
        for n, d in enumerate((1, 3, 2)):
            owner = lax.rem(t + d, TP)
            finish(owner * 2 + half, ho.at[half, n])
            cp = remote(
                ho.at[half, n], g.at[t, half], a_s.at[half, n], a_r.at[half, d - 1], (s, owner)
            )
            cp.start()
            sent[half, n] = cp
        finish(t * 2 + half, g.at[t, half])

    @pl.when(core == 0)
    def _():
        fwd.wait_send()

    for cp in wb:
        cp.wait()
    src = wf.at[1:4, :, :, core]
    wc = remote(src, src, wc_s, wc_r, (sib, t))
    wc.start()
    wocopy.wait()
    wc.wait()

    results = []
    own = []
    for half in range(2):
        for d in range(1, TP):
            remote(
                ho.at[half, 0], g.at[lax.rem(t + TP - d, TP), half], a_s.at[half, 0], a_r.at[half, d - 1], xpeer(d)
            ).wait_recv()
        for n, d in enumerate((1, 3, 2, 0)):
            acc = jnp.zeros((C, 512), F32)
            for p in range(TP):
                acc = acc + jnp.dot(
                    g[p, half], wf[d, p].reshape(512, 512), preferred_element_type=F32
                )
            ob[half, n] = acc.astype(BF16)
            rows = out_ref.at[pl.ds(pl.multiple_of(t * 512 + half * C, C), C)]
            if d:
                cp = remote(ob.at[half, n], rows, b_s.at[half, n], b_r.at[half, d - 1], xpeer(d))
                cp.start()
                results.append(cp)
            else:
                cp = pltpu.make_async_copy(ob.at[half, n], rows, own_s.at[half])
                cp.start()
                own.append(cp)

    for cp in sent.values():
        cp.wait_send()
    for cp in results:
        cp.wait_send()
    for half in range(2):
        for d in range(1, TP):
            src_t = lax.rem(t + TP - d, TP)
            rows = out_ref.at[pl.ds(pl.multiple_of(src_t * 512 + half * C, C), C)]
            remote(ob.at[half, 0], rows, b_s.at[half, 0], b_r.at[half, d - 1], xpeer(d)).wait_recv()
    for cp in own:
        cp.wait()


def body(tokens, gain, w_in, conv_taps, w_out):
    wt = jnp.transpose(w_in, (1, 2, 0)).reshape(HL * 160, D)
    eq, ek = feature_maps()
    hbm = pl.BlockSpec(memory_space=pl.ANY)
    vmem = pl.BlockSpec(memory_space=pltpu.VMEM)
    dma = pltpu.SemaphoreType.DMA
    return pl.pallas_call(
        kernel,
        out_shape=jax.ShapeDtypeStruct((T, 512), BF16),
        in_specs=[hbm, vmem, hbm, vmem, hbm, hbm, hbm],
        out_specs=hbm,
        scratch_shapes=[
            pltpu.VMEM((T, D), BF16),
            pltpu.VMEM((HL * 160, D), BF16),
            pltpu.VMEM((2, FP, HL * FP), BF16),
            pltpu.VMEM((2, HL * F, FP), BF16),
            pltpu.VMEM((8, VW + QW), F32),
            pltpu.VMEM((8 + T, VW + QW), F32),
            pltpu.VMEM((T, VW), BF16),
            pltpu.VMEM((T, QW), BF16),
            pltpu.VMEM((NC, QW, C), BF16),
            pltpu.VMEM((NC, HL * F, DV), F32),
            pltpu.VMEM((T, VW), F32),
            pltpu.VMEM((T, HL * FP), BF16),
            pltpu.VMEM((CHIPS, ROWS, DV), BF16),
            pltpu.VMEM((SEQ, ROWS, DV), BF16),
            pltpu.VMEM((CHIPS, 2, ROWS, DV), BF16),
            pltpu.VMEM((CHIPS, 2, ROWS, DV), BF16),
            pltpu.VMEM((HL, FP, DV), BF16),
            pltpu.VMEM((4, 4, 4, 2, 64, 512), BF16),
            pltpu.VMEM((2, 3, C, VW), BF16),
            pltpu.VMEM((TP, 2, C, VW), BF16),
            pltpu.VMEM((2, 4, C, 512), BF16),
            dma((3,)), dma((NC,)), dma, dma, dma, dma, dma, dma, dma, dma, dma,
            dma((3,)), dma((3,)), dma((6,)), dma((6,)), dma((6,)), dma((6,)), dma, dma,
            dma((2, 3)), dma((2, 3)), dma((2, 4)), dma((2, 3)), dma((2,)),
        ],
        compiler_params=pltpu.CompilerParams(
            collective_id=0, has_side_effects=True, vmem_limit_bytes=60 * 1024 * 1024
        ),
    )(
        tokens, gain.reshape(1, D), wt, conv_taps, w_out.reshape(4, 4, 2, 64, 512),
        jnp.asarray(eq), jnp.asarray(ek),
    )


def solution(mesh):
    return jax.shard_map(
        body,
        mesh=mesh,
        in_specs=(P("seq", None), P(), P(None, "tp", None), P(None, "tp", None), P(None, "tp")),
        out_specs=P("seq", "tp"),
        check_vma=False,
    )
```

time: 313 us -> 95.9 us (0.31)
  the two profiles are of different devices: /device:TPU:1 before, /device:TPU:25 now
where the time goes in v1:
time: 95.9 us; the launch traced here: 95.7 us
  Pallas kernels  91.3 us (95%)
  local copies, waits for them, and re-layouts  4.34 us (5%)
    pallas_call x1, Pallas kernels, body(): pl.pallas_call(kernel, out_shape=jax.ShapeDtypeStruct((T, 512), BF16), in...  91.3 us
    unnamed x1, local copies, waits for them, and re-layouts  3.05 us

profile of v1, /device:TPU:25, one launch (start us, length us, event | category | flops | bytes accessed | tf_op | source)
XLA Modules:
  0.0 95.7 jit_solution(12983215387450448314)
XLA Ops:
  0.0 1.3 %reshape.9.gain_ref = bf16[1,2048]{1,0:T(2,128)(2,1)} reshape(bf16[2048]{0:T(1024)(128)(2,1)} %param.8) | data formatting | bytes 8192 | tf_op jit(solution)/shard_map/reshape | solution.py:428
  1.3 91.3 %shard_map.73 = bf16[2048,512]{1,0:T(8,128)(2,1)} custom-call(bf16[2048,2048]{1,0:T(8,128)(2,1)} %x_hbm.1, bf16[1,2048]{1,0:T(2,128)(2,1)} %reshape.9.gain_ref, bf16[640,2048]{1,0:T(8,128)(2,1)} %bitcast.4, bf16[3,4,160]{2,1,0:T(4,128)(2,1)} %taps_ref.1, bf16[4,4,2,64,512]{4,3,2,1,0:T(8,128)(2,1)} %bitcast.5, bf16[2,256,1024]{2,1,0:T(8,128)(2,1)} %constant.4.clone.eq_hbm, ...), custom_call_target="tpu_custom_call" | custom-call | tf_op jit(solution)/shard_map/pallas_call | solution.py:393
  92.6 3.0 %copy.9 = bf16[2048,512]{1,0:T(8,128)(2,1)} copy(bf16[2048,512]{1,0:T(8,128)(2,1)} %shard_map.73) | data formatting | bytes 4194304

commit v2 on v1

v2 whole, which is shorter than its diff:
```python
import functools
import math

import jax
import jax.numpy as jnp
import numpy as np
from jax import lax
from jax.experimental import pallas as pl
from jax.experimental.pallas import tpu as pltpu
from jax.sharding import PartitionSpec as P

DK = 16
DV = 128
HL = 4
T = 2048
D = 2048
C = 256
NC = T // C
F = 160
FP = 256
VW = HL * DV
QW = HL * 2 * DK
SEQ = 32
TP = 4
CHIPS = SEQ // 2
ROWS = HL * F // CHIPS
EPS = 1e-06
MESH = pl.DeviceIdType.MESH
F32 = jnp.float32
BF16 = jnp.bfloat16


def feature_maps():
    eq = np.zeros((2, FP, HL * FP), np.float32)
    ek = np.zeros((2, HL * F, FP), np.float32)
    one = QW
    for h in range(HL):
        q0, k0 = 2 * DK * h, 2 * DK * h + DK
        f = 0
        for i in range(DK):
            for j in range(i, DK):
                eq[0, q0 + i, h * FP + f] = (1.0 if i == j else 2.0) / 32.0
                eq[1, q0 + j, h * FP + f] = 1.0
                ek[0, h * F + f, k0 + i] = 1.0
                ek[1, h * F + f, k0 + j] = 1.0
                f += 1
        for i in range(DK):
            eq[0, q0 + i, h * FP + f] = 0.25
            eq[1, one, h * FP + f] = 1.0
            ek[0, h * F + f, k0 + i] = 1.0
            ek[1, h * F + f, one] = 1.0
            f += 1
        eq[0, one, h * FP + f] = 1.0
        eq[1, one, h * FP + f] = 1.0
        ek[0, h * F + f, one] = 1.0
        ek[1, h * F + f, one] = 1.0
    return eq.astype(jnp.bfloat16), ek.astype(jnp.bfloat16)


def kernel(
    x_hbm, gain_ref, wt_hbm, taps_ref, wo_hbm, eq_hbm, ek_hbm,
    out_ref,
    xv, xt8, wv, wg, eqv, ekv, taps, pf, tl, mx, ga, sc, nl, fq, sb, r1, p2, r2, ps, pp, wf, gh, ob,
    in_sem, x_sem, wo_sem, halo_s, halo_r, s1_s, s1_r, s2_s, s2_r, s3_s, s3_r,
    wx_s, wx_r, wa_s, wa_r, wb_s, wb_r, wc_s, wc_r, a_s, a_r, q_s, q_r, b_s, b_r, own_s,
):
    s = lax.axis_index("seq")
    t = lax.axis_index("tp")
    chip = s // 2
    core = s % 2
    zc = s // 8
    yc = (s // 2) % 4
    sib = s + 1 - 2 * core

    def remote(src, dst, ss, rs, dev):
        return pltpu.make_async_remote_copy(
            src_ref=src, dst_ref=dst, send_sem=ss, recv_sem=rs, device_id=dev, device_id_type=MESH
        )

    def near(d):
        return lax.rem(t + d, TP)

    def xpeer(d):
        return (s, near(d))

    def ypeer(d):
        return (zc * 8 + lax.rem(yc + d, 4) * 2 + core, t)

    def zpeer(d):
        return (lax.rem(zc + d, 4) * 8 + yc * 2 + core, t)

    tiles = [(d, half) for half in (1, 0) for d in (1, 3, 2)] + [(0, 1), (0, 0)]

    wcopy = pltpu.make_async_copy(wt_hbm, wv, in_sem.at[0])
    wcopy.start()
    tcopies = []
    for c in range(NC):
        cp = pltpu.make_async_copy(x_hbm.at[pl.ds(c * C + C - 8, 8)], xt8.at[pl.ds(8 * c, 8)], in_sem.at[3 + c])
        cp.start()
        tcopies.append(cp)
    xcopies = []
    for i, (d, half) in enumerate(tiles):
        base = pl.multiple_of((near(d) * 2 + half) * C, C)
        cp = pltpu.make_async_copy(x_hbm.at[pl.ds(base, C)], xv.at[i], x_sem.at[i])
        cp.start()
        xcopies.append(cp)
    ekcopy = pltpu.make_async_copy(ek_hbm, ekv, in_sem.at[1])
    ekcopy.start()
    eqcopy = pltpu.make_async_copy(eq_hbm, eqv, in_sem.at[2])
    eqcopy.start()
    wocopy = pltpu.make_async_copy(wo_hbm, wf.at[0], wo_sem)
    wocopy.start()

    barrier = pltpu.get_barrier_semaphore()

    def greet(j, carry):
        pl.semaphore_signal(barrier, inc=1, device_id=(lax.rem(s + j, SEQ), t), device_id_type=MESH)
        return carry

    lax.fori_loop(1, SEQ, greet, 0)
    for d in range(1, TP):
        pl.semaphore_signal(barrier, inc=1, device_id=xpeer(d), device_id_type=MESH)

    pp[:, :, F:, :] = jnp.zeros((TP, HL, FP - F, DV), BF16)

    row = lax.broadcasted_iota(jnp.int32, (160, 128), 0)
    col = lax.broadcasted_iota(jnp.int32, (160, 128), 1)
    pick_v = (row == col + 2 * DK).astype(F32).astype(BF16)
    for k in range(3):
        tk = taps_ref[k]
        tv = jnp.dot(tk, pick_v, preferred_element_type=F32)
        tq = jnp.zeros((1, QW), F32)
        for h in range(HL):
            taps[k : k + 1, h * DV : (h + 1) * DV] = tv[h : h + 1, :]
            pick_q = ((row + 2 * DK * h == col) & (row < 2 * DK)).astype(F32).astype(BF16)
            tq = tq + jnp.dot(tk, pick_q, preferred_element_type=F32)[h : h + 1, :]
        taps[k : k + 1, VW:] = tq

    wcopy.wait()
    gain = gain_ref[...].astype(F32)
    for h in range(HL):
        for r in range(0, 160, 32):
            dst = VW + 32 * h if r == 0 else h * DV + r - 32
            src = h * 160 + r
            wg[dst : dst + 32, :] = (wv[src : src + 32, :].astype(F32) * gain).astype(BF16)

    def project(xt):
        xf = xt.astype(F32)
        scale = lax.rsqrt(jnp.mean(xf * xf, axis=-1, keepdims=True) + EPS)
        pr = lax.dot_general(xt, wg[...], (((1,), (1,)), ((), ())), preferred_element_type=F32)
        return (pr * scale).astype(BF16).astype(F32)

    for cp in tcopies:
        cp.wait()
    tl[8:, :] = project(xt8[...])

    pl.semaphore_wait(barrier, SEQ - 1 + TP - 1)
    halo = remote(tl.at[pl.ds(8 * NC, 8)], tl.at[pl.ds(0, 8)], halo_s, halo_r, (lax.rem(s + 1, SEQ), t))
    halo.start()
    wx = []
    for d in range(1, TP):
        cp = remote(
            wo_hbm.at[zc, yc, core], wf.at[TP - d, zc, yc, core], wx_s.at[d - 1], wx_r.at[d - 1], xpeer(d)
        )
        cp.start()
        wx.append(cp)

    def mix(i, c, dst):
        buf = pf.at[i % 2]
        buf[0:8, :] = tl[pl.ds(pl.multiple_of(c * 8, 8), 8), :]
        buf[8:, :] = project(xv[i])
        mixed = (
            buf[6 : 6 + C, :] * taps[0:1, :] + buf[7 : 7 + C, :] * taps[1:2, :] + buf[8 : 8 + C, :] * taps[2:3, :]
        )
        dst[...] = mixed.astype(BF16)

    def states(c, src):
        qe = jnp.concatenate(
            [jnp.transpose(src[:, VW:].astype(F32)).astype(BF16), jnp.ones((FP - QW, C), BF16)], axis=0
        )
        fk = (
            jnp.dot(ekv[0], qe, preferred_element_type=F32) * jnp.dot(ekv[1], qe, preferred_element_type=F32)
        ).astype(BF16)
        for h in range(HL):
            sc[c, h * F : (h + 1) * F, :] = jnp.dot(
                fk[h * F : (h + 1) * F, :], src[:, h * DV : (h + 1) * DV], preferred_element_type=F32
            )

    ekcopy.wait()
    sent = []
    wa = []
    for i, (d, half) in enumerate(tiles):
        c = near(d) * 2 + half
        if i == 3:
            halo.wait()
            tl[0:8, :] = jnp.where(s == 0, 0.0, tl[0:8, :])
        if i == 4:
            for cp in wx:
                cp.wait()
            for n in range(1, 4):
                src = wf.at[1:4, zc, yc, core, :, 0:256]
                cp = remote(src, src, wa_s.at[n - 1], wa_r.at[n - 1], ypeer(n))
                cp.start()
                wa.append(cp)
                src = wf.at[1:4, zc, yc, core, :, 256:512]
                cp = remote(src, src, wa_s.at[n + 2], wa_r.at[n + 2], zpeer(n))
                cp.start()
                wa.append(cp)
        xcopies[i].wait()
        tile = mx.at[i] if d else ga.at[t, half]
        mix(i, c, tile)
        if d:
            cp = remote(tile, ga.at[t, half], a_s.at[half, d - 1], a_r.at[half, d - 1], xpeer(d))
            cp.start()
            sent.append(cp)
        states(c, tile)

    run = jnp.zeros((HL * F, DV), F32)
    for c in range(NC):
        part = sc[c]
        if c % 2 == 0:
            sc[c] = run
        run = run + part
    for k in range(CHIPS):
        sb[k] = run[k * ROWS : (k + 1) * ROWS, :].astype(BF16)

    def spread(i, carry):
        k = lax.rem(chip + i, CHIPS)
        remote(sb.at[k], r1.at[s], s1_s, s1_r, (2 * k, t)).start()
        return carry

    lax.fori_loop(1, CHIPS, spread, 0)

    @pl.when(core == 1)
    def _():
        cp = remote(sb.at[chip], r1.at[s], s3_s, s1_r, (s - 1, t))
        cp.start()
        cp.wait_send()

    @pl.when(core == 0)
    def _():
        r1[s] = sb[chip]

    for cp in wa:
        cp.wait()
    wb = []
    for d in range(1, 4):
        src = wf.at[1:4, zc, :, core, :, 0:256]
        cp = remote(src, src, wb_s.at[d - 1], wb_r.at[d - 1], zpeer(d))
        cp.start()
        wb.append(cp)
        src = wf.at[1:4, :, yc, core, :, 256:512]
        cp = remote(src, src, wb_s.at[d + 2], wb_r.at[d + 2], ypeer(d))
        cp.start()
        wb.append(cp)

    eqcopy.wait()
    pos = lax.broadcasted_iota(jnp.int32, (C, C), 0) >= lax.broadcasted_iota(jnp.int32, (C, C), 1)

    def arrived(d, half):
        n = TP - d - 1
        remote(mx.at[0], ga.at[near(d), half], a_s.at[half, n], a_r.at[half, n], xpeer(d)).wait_recv()

    def scores(q, kt, h):
        parts = []
        if h > 0:
            parts.append(jnp.zeros((32 * h, C), BF16))
        parts.append(kt[32 * h + 16 : 32 * h + 32, :])
        parts.append(jnp.zeros((QW - 32 * h - 16, C), BF16))
        up = jnp.dot(q, jnp.concatenate(parts, axis=0), preferred_element_type=F32) + 1.0
        return up * up * 0.5 + 0.5

    def keys(src):
        return (jnp.transpose(src[:, VW:].astype(F32)) * 0.25).astype(BF16)

    def local(d, half):
        src = ga.at[near(d), half]
        q = src[:, VW:]
        qe = jnp.concatenate([q, jnp.ones((C, FP - QW), BF16)], axis=1)
        kt = keys(src)
        for h in range(HL):
            fq[half, d, :, h * FP : (h + 1) * FP] = (
                jnp.dot(qe, eqv[0, :, h * FP : (h + 1) * FP], preferred_element_type=F32)
                * jnp.dot(qe, eqv[1, :, h * FP : (h + 1) * FP], preferred_element_type=F32)
            ).astype(BF16)
            w = jnp.where(pos, scores(q, kt, h), 0.0).astype(BF16)
            nl[half, d, :, h * DV : (h + 1) * DV] = jnp.dot(
                w, src[:, h * DV : (h + 1) * DV], preferred_element_type=F32
            )

    def across(d):
        q = ga[near(d), 1, :, VW:]
        src = ga.at[near(d), 0]
        kt = keys(src)
        for h in range(HL):
            w = scores(q, kt, h).astype(BF16)
            nl[1, d, :, h * DV : (h + 1) * DV] += jnp.dot(
                w, src[:, h * DV : (h + 1) * DV], preferred_element_type=F32
            )

    local(0, 1)
    local(0, 0)
    across(0)

    @pl.when(core == 0)
    def _():
        pltpu.make_async_copy(r1.at[0 : SEQ - 1], r1.at[0 : SEQ - 1], s1_r).wait()
        acc = jnp.zeros((ROWS, DV), F32)
        for k in range(SEQ):
            p2[k // 2, k % 2] = acc.astype(BF16)
            acc = acc + r1[k].astype(F32)
        r2[chip] = p2[chip]

        def back(i, carry):
            k = lax.rem(chip + i, CHIPS)
            remote(p2.at[k], r2.at[chip], s2_s, s2_r, (2 * k, t)).start()
            return carry

        lax.fori_loop(1, CHIPS, back, 0)

    pltpu.make_async_copy(sb.at[0 : CHIPS - 1], sb.at[0 : CHIPS - 1], s1_s).wait()
    for d in (3, 1, 2):
        arrived(d, 1)
        local(d, 1)

    fwd = remote(r2, r2, s3_s, s3_r, (sib, t))

    @pl.when(core == 0)
    def _():
        pltpu.make_async_copy(p2.at[0 : CHIPS - 1], p2.at[0 : CHIPS - 1], s2_s).wait()
        pltpu.make_async_copy(r2.at[0 : CHIPS - 1], r2.at[0 : CHIPS - 1], s2_r).wait()
        fwd.start()

    @pl.when(core == 1)
    def _():
        fwd.wait_recv()

    pcopies = []
    for d in (1, 3, 2, 0):
        n = near(d)
        for k in range(CHIPS):
            h, o = k // 4, (k % 4) * ROWS
            val = (r2[k, core].astype(F32) + sc[2 * n, k * ROWS : (k + 1) * ROWS, :]).astype(BF16)
            if d:
                ps[d - 1, h, o : o + ROWS, :] = val
            else:
                pp[t, h, o : o + ROWS, :] = val
        if d:
            cp = remote(ps.at[d - 1], pp.at[t, :, 0:F, :], q_s.at[d - 1], q_r.at[d - 1], xpeer(d))
            cp.start()
            pcopies.append(cp)

    for d in (3, 1, 2):
        arrived(d, 0)
        local(d, 0)
        across(d)

    @pl.when(core == 0)
    def _():
        fwd.wait_send()

    for cp in wb:
        cp.wait()
    src = wf.at[1:4, :, :, core]
    wc = remote(src, src, wc_s, wc_r, (sib, t))
    wc.start()
    for cp in pcopies:
        cp.wait()

    results = []
    own = []
    for half in range(2):
        for d in range(TP):
            for h in range(HL):
                num = nl[half, d, :, h * DV : (h + 1) * DV] + jnp.dot(
                    fq[half, d, :, h * FP : (h + 1) * FP], pp[near(d), h], preferred_element_type=F32
                )
                spread_ = jnp.mean(num * num, axis=-1, keepdims=True)
                gh[half, d, :, h * DV : (h + 1) * DV] = (num * lax.rsqrt(spread_ + EPS)).astype(BF16)
        if half == 0:
            wocopy.wait()
            wc.wait()
        for n, d in enumerate((1, 3, 2, 0)):
            acc = jnp.zeros((C, 512), F32)
            for p in range(TP):
                acc = acc + jnp.dot(
                    gh[half, p], wf[d, near(p)].reshape(512, 512), preferred_element_type=F32
                )
            ob[half, n] = acc.astype(BF16)
            rows = out_ref.at[pl.ds(pl.multiple_of(t * 512 + half * C, C), C)]
            if d:
                cp = remote(ob.at[half, n], rows, b_s.at[half, d - 1], b_r.at[half, d - 1], xpeer(d))
                cp.start()
                results.append(cp)
            else:
                cp = pltpu.make_async_copy(ob.at[half, n], rows, own_s.at[half])
                cp.start()
                own.append(cp)

    for cp in sent + results:
        cp.wait_send()
    for half in range(2):
        for d in range(1, TP):
            rows = out_ref.at[pl.ds(pl.multiple_of(near(TP - d) * 512 + half * C, C), C)]
            remote(ob.at[half, 0], rows, b_s.at[half, 0], b_r.at[half, d - 1], xpeer(d)).wait_recv()
    for cp in own:
        cp.wait()


def body(tokens, gain, w_in, conv_taps, w_out):
    wt = jnp.transpose(w_in, (1, 2, 0)).reshape(HL * 160, D)
    eq, ek = feature_maps()
    hbm = pl.BlockSpec(memory_space=pl.ANY)
    vmem = pl.BlockSpec(memory_space=pltpu.VMEM)
    dma = pltpu.SemaphoreType.DMA
    width = VW + QW
    return pl.pallas_call(
        kernel,
        out_shape=jax.ShapeDtypeStruct((T, 512), BF16),
        in_specs=[hbm, vmem, hbm, vmem, hbm, hbm, hbm],
        out_specs=hbm,
        scratch_shapes=[
            pltpu.VMEM((NC, C, D), BF16),
            pltpu.VMEM((8 * NC, D), BF16),
            pltpu.VMEM((width, D), BF16),
            pltpu.VMEM((width, D), BF16),
            pltpu.VMEM((2, FP, HL * FP), BF16),
            pltpu.VMEM((2, HL * F, FP), BF16),
            pltpu.VMEM((8, width), F32),
            pltpu.VMEM((2, 8 + C, width), F32),
            pltpu.VMEM((8 + 8 * NC, width), F32),
            pltpu.VMEM((6, C, width), BF16),
            pltpu.VMEM((TP, 2, C, width), BF16),
            pltpu.VMEM((NC, HL * F, DV), F32),
            pltpu.VMEM((2, TP, C, VW), F32),
            pltpu.VMEM((2, TP, C, HL * FP), BF16),
            pltpu.VMEM((CHIPS, ROWS, DV), BF16),
            pltpu.VMEM((SEQ, ROWS, DV), BF16),
            pltpu.VMEM((CHIPS, 2, ROWS, DV), BF16),
            pltpu.VMEM((CHIPS, 2, ROWS, DV), BF16),
            pltpu.VMEM((3, HL, F, DV), BF16),
            pltpu.VMEM((TP, HL, FP, DV), BF16),
            pltpu.VMEM((4, 4, 4, 2, 64, 512), BF16),
            pltpu.VMEM((2, TP, C, VW), BF16),
            pltpu.VMEM((2, 4, C, 512), BF16),
            dma((3 + NC,)), dma((NC,)), dma, dma, dma, dma, dma, dma, dma, dma, dma,
            dma((3,)), dma((3,)), dma((6,)), dma((6,)), dma((6,)), dma((6,)), dma, dma,
            dma((2, 3)), dma((2, 3)), dma((3,)), dma((3,)), dma((2, 3)), dma((2, 3)), dma((2,)),
        ],
        compiler_params=pltpu.CompilerParams(
            collective_id=0, has_side_effects=True, vmem_limit_bytes=60 * 1024 * 1024
        ),
    )(
        tokens, gain.reshape(1, D), wt, conv_taps, w_out.reshape(4, 4, 2, 64, 512),
        jnp.asarray(eq), jnp.asarray(ek),
    )


def solution(mesh):
    return jax.shard_map(
        body,
        mesh=mesh,
        in_specs=(P("seq", None), P(), P(None, "tp", None), P(None, "tp", None), P(None, "tp")),
        out_specs=P("seq", "tp"),
        check_vma=False,
    )
```

time: 95.9 us -> 92.4 us (0.964)
  the two profiles are of different devices: /device:TPU:25 before, /device:TPU:1 now
where the time goes in v2:
time: 92.4 us; the launch traced here: 92.2 us
  Pallas kernels  87.9 us (95%)
  local copies, waits for them, and re-layouts  4.34 us (5%)
    pallas_call x1, Pallas kernels, body(): pl.pallas_call(kernel, out_shape=jax.ShapeDtypeStruct((T, 512), BF16), in...  87.9 us
    unnamed x1, local copies, waits for them, and re-layouts  3.05 us

profile of v2, /device:TPU:1, one launch (start us, length us, event | category | flops | bytes accessed | tf_op | source)
XLA Modules:
  0.0 92.2 jit_solution(14618582855439923979)
XLA Ops:
  0.0 1.3 %reshape.9.gain_ref = bf16[1,2048]{1,0:T(2,128)(2,1)} reshape(bf16[2048]{0:T(1024)(128)(2,1)} %param.8) | data formatting | bytes 8192 | tf_op jit(solution)/shard_map/reshape | solution.py:454
  1.3 87.9 %shard_map.73 = bf16[2048,512]{1,0:T(8,128)(2,1)} custom-call(bf16[2048,2048]{1,0:T(8,128)(2,1)} %x_hbm.1, bf16[1,2048]{1,0:T(2,128)(2,1)} %reshape.9.gain_ref, bf16[640,2048]{1,0:T(8,128)(2,1)} %bitcast.4, bf16[3,4,160]{2,1,0:T(4,128)(2,1)} %taps_ref.1, bf16[4,4,2,64,512]{4,3,2,1,0:T(8,128)(2,1)} %bitcast.5, bf16[2,256,1024]{2,1,0:T(8,128)(2,1)} %constant.4.clone.eq_hbm, ...), custom_call_target="tpu_custom_call" | custom-call | tf_op jit(solution)/shard_map/pallas_call | solution.py:417
  89.2 3.0 %copy.9 = bf16[2048,512]{1,0:T(8,128)(2,1)} copy(bf16[2048,512]{1,0:T(8,128)(2,1)} %shard_map.73) | data formatting | bytes 4194304

commit v3 on v2

--- a/solution.py
+++ b/solution.py
@@ -137,7 +137,7 @@
         taps[k : k + 1, VW:] = tq
 
     wcopy.wait()
-    gain = gain_ref[...].astype(F32)
+    gain = gain_ref[...].astype(F32)[None, :]
     for h in range(HL):
         for r in range(0, 160, 32):
             dst = VW + 32 * h if r == 0 else h * DV + r - 32
@@ -189,12 +189,13 @@
     ekcopy.wait()
     sent = []
     wa = []
+    wb = []
     for i, (d, half) in enumerate(tiles):
         c = near(d) * 2 + half
         if i == 3:
             halo.wait()
             tl[0:8, :] = jnp.where(s == 0, 0.0, tl[0:8, :])
-        if i == 4:
+        if i == 2:
             for cp in wx:
                 cp.wait()
             for n in range(1, 4):
@@ -206,6 +207,18 @@
                 cp = remote(src, src, wa_s.at[n + 2], wa_r.at[n + 2], zpeer(n))
                 cp.start()
                 wa.append(cp)
+        if i == 6:
+            for cp in wa:
+                cp.wait()
+            for n in range(1, 4):
+                src = wf.at[1:4, zc, :, core, :, 0:256]
+                cp = remote(src, src, wb_s.at[n - 1], wb_r.at[n - 1], zpeer(n))
+                cp.start()
+                wb.append(cp)
+                src = wf.at[1:4, :, yc, core, :, 256:512]
+                cp = remote(src, src, wb_s.at[n + 2], wb_r.at[n + 2], ypeer(n))
+                cp.start()
+                wb.append(cp)
         xcopies[i].wait()
         tile = mx.at[i] if d else ga.at[t, half]
         mix(i, c, tile)
@@ -233,26 +246,11 @@
 
     @pl.when(core == 1)
     def _():
-        cp = remote(sb.at[chip], r1.at[s], s3_s, s1_r, (s - 1, t))
-        cp.start()
-        cp.wait_send()
+        remote(sb.at[chip], r1.at[s], s3_s, s1_r, (s - 1, t)).start()
 
     @pl.when(core == 0)
     def _():
         r1[s] = sb[chip]
-
-    for cp in wa:
-        cp.wait()
-    wb = []
-    for d in range(1, 4):
-        src = wf.at[1:4, zc, :, core, :, 0:256]
-        cp = remote(src, src, wb_s.at[d - 1], wb_r.at[d - 1], zpeer(d))
-        cp.start()
-        wb.append(cp)
-        src = wf.at[1:4, :, yc, core, :, 256:512]
-        cp = remote(src, src, wb_s.at[d + 2], wb_r.at[d + 2], ypeer(d))
-        cp.start()
-        wb.append(cp)
 
     eqcopy.wait()
     pos = lax.broadcasted_iota(jnp.int32, (C, C), 0) >= lax.broadcasted_iota(jnp.int32, (C, C), 1)
@@ -333,6 +331,7 @@
 
     @pl.when(core == 1)
     def _():
+        remote(sb.at[chip], r1.at[s], s3_s, s1_r, (s - 1, t)).wait_send()
         fwd.wait_recv()
 
     pcopies = []
@@ -448,10 +447,10 @@
             dma((2, 3)), dma((2, 3)), dma((3,)), dma((3,)), dma((2, 3)), dma((2, 3)), dma((2,)),
         ],
         compiler_params=pltpu.CompilerParams(
-            collective_id=0, has_side_effects=True, vmem_limit_bytes=60 * 1024 * 1024
+            collective_id=0, has_side_effects=True, vmem_limit_bytes=50 * 1024 * 1024
         ),
     )(
-        tokens, gain.reshape(1, D), wt, conv_taps, w_out.reshape(4, 4, 2, 64, 512),
+        tokens, gain, wt, conv_taps, w_out.reshape(4, 4, 2, 64, 512),
         jnp.asarray(eq), jnp.asarray(ek),
     )
 

time: 92.4 us -> 93.7 us (1.014)
    unnamed x1 -> x9, local copies, waits for them, and re-layouts: 3.05 us -> 5.01 us
    reshape x1 -> x0, local copies, waits for them, and re-layouts: 1.29 us -> none  [body(): gain.reshape(1, D)]
where the time goes in v3:
time: 93.7 us; the launch traced here: 93.5 us
  Pallas kernels  88.5 us (94%)
  local copies, waits for them, and re-layouts  5.01 us (5%)
    pallas_call x1, Pallas kernels, body(): pl.pallas_call(kernel, out_shape=jax.ShapeDtypeStruct((T, 512), BF16), in...  88.5 us
    unnamed x9, local copies, waits for them, and re-layouts  5.01 us

profile of v3, /device:TPU:1, one launch (start us, length us, event | category | flops | bytes accessed | tf_op | source)
XLA Modules:
  0.0 93.5 jit_solution(14193912660863975784)
XLA Ops:
  0.0 0.0 copy-start
  0.0 1.2 %copy-done = bf16[2,256,1024]{2,1,0:T(8,128)(2,1)S(1)} copy-done((bf16[2,256,1024]{2,1,0:T(8,128)(2,1)S(1)}, bf16[2,256,1024]{2,1,0:T(8,128)(2,1)}, u32[]{:S(2)}) %copy-start) | copy-done | bytes 1048600
  1.2 0.0 copy-start.1
  1.2 1.1 %copy-done.1 = bf16[2,640,256]{2,1,0:T(8,128)(2,1)S(1)} copy-done((bf16[2,640,256]{2,1,0:T(8,128)(2,1)S(1)}, bf16[2,640,256]{2,1,0:T(8,128)(2,1)}, u32[]{:S(2)}) %copy-start.1) | copy-done | bytes 655384
  2.3 0.0 copy-start.2
  2.3 0.7 copy-done.2
  3.0 0.0 copy-start.3
  3.0 0.7 copy-done.3
  3.7 88.5 %shard_map.73 = bf16[2048,512]{1,0:T(8,128)(2,1)S(1)} custom-call(bf16[2048,2048]{1,0:T(8,128)(2,1)} %x_hbm.1, bf16[2048]{0:T(1024)(128)(2,1)S(1)} %copy-done.3, bf16[640,2048]{1,0:T(8,128)(2,1)} %bitcast.4, bf16[3,4,160]{2,1,0:T(4,128)(2,1)S(1)} %copy-done.2, bf16[4,4,2,64,512]{4,3,2,1,0:T(8,128)(2,1)} %bitcast.5, bf16[2,256,1024]{2,1,0:T(8,128)(2,1)S(1)} %copy-done, ...), custom_call_target="tpu_custom_call" | custom-call | tf_op jit(solution)/shard_map/pallas_call | solution.py:416
  92.2 1.3 %copy.9 = bf16[2048,512]{1,0:T(8,128)(2,1)} copy(bf16[2048,512]{1,0:T(8,128)(2,1)S(1)} %shard_map.73) | data formatting | bytes 4194304
Async XLA Ops:
  0.0 1.2 %copy-start = (bf16[2,256,1024]{2,1,0:T(8,128)(2,1)S(1)}, bf16[2,256,1024]{2,1,0:T(8,128)(2,1)}, u32[]{:S(2)}) copy-start(bf16[2,256,1024]{2,1,0:T(8,128)(2,1)} %constant.4.clone.eq_hbm) | copy-start | bytes 3145732
  1.2 1.1 %copy-start.1 = (bf16[2,640,256]{2,1,0:T(8,128)(2,1)S(1)}, bf16[2,640,256]{2,1,0:T(8,128)(2,1)}, u32[]{:S(2)}) copy-start(bf16[2,640,256]{2,1,0:T(8,128)(2,1)} %constant.5.clone.ek_hbm) | copy-start | bytes 1966084
  2.3 0.7 copy-start.2
  3.0 0.7 copy-start.3

commit v4 on v3

--- a/solution.py
+++ b/solution.py
@@ -186,10 +186,32 @@
                 fk[h * F : (h + 1) * F, :], src[:, h * DV : (h + 1) * DV], preferred_element_type=F32
             )
 
-    ekcopy.wait()
     sent = []
     wa = []
-    wb = []
+    wb = {1: [], 2: [], 3: []}
+
+    def onward(shard):
+        n = 6 * (shard - 1)
+        for d in range(1, 4):
+            src = wf.at[shard, zc, :, core, :, 0:256]
+            cp = remote(src, src, wb_s.at[n], wb_r.at[n], zpeer(d))
+            cp.start()
+            wb[shard].append(cp)
+            src = wf.at[shard, :, yc, core, :, 256:512]
+            cp = remote(src, src, wb_s.at[n + 1], wb_r.at[n + 1], ypeer(d))
+            cp.start()
+            wb[shard].append(cp)
+            n += 2
+
+    def across_cores(shard):
+        for cp in wb[shard]:
+            cp.wait()
+        src = wf.at[shard, :, :, core]
+        cp = remote(src, src, wc_s.at[shard - 1], wc_r.at[shard - 1], (sib, t))
+        cp.start()
+        return cp
+
+    ekcopy.wait()
     for i, (d, half) in enumerate(tiles):
         c = near(d) * 2 + half
         if i == 3:
@@ -207,18 +229,10 @@
                 cp = remote(src, src, wa_s.at[n + 2], wa_r.at[n + 2], zpeer(n))
                 cp.start()
                 wa.append(cp)
-        if i == 6:
+        if i == 5:
             for cp in wa:
                 cp.wait()
-            for n in range(1, 4):
-                src = wf.at[1:4, zc, :, core, :, 0:256]
-                cp = remote(src, src, wb_s.at[n - 1], wb_r.at[n - 1], zpeer(n))
-                cp.start()
-                wb.append(cp)
-                src = wf.at[1:4, :, yc, core, :, 256:512]
-                cp = remote(src, src, wb_s.at[n + 2], wb_r.at[n + 2], ypeer(n))
-                cp.start()
-                wb.append(cp)
+            onward(1)
         xcopies[i].wait()
         tile = mx.at[i] if d else ga.at[t, half]
         mix(i, c, tile)
@@ -348,6 +362,9 @@
             cp = remote(ps.at[d - 1], pp.at[t, :, 0:F, :], q_s.at[d - 1], q_r.at[d - 1], xpeer(d))
             cp.start()
             pcopies.append(cp)
+    wc = {1: across_cores(1)}
+    onward(3)
+    onward(2)
 
     for d in (3, 1, 2):
         arrived(d, 0)
@@ -358,11 +375,6 @@
     def _():
         fwd.wait_send()
 
-    for cp in wb:
-        cp.wait()
-    src = wf.at[1:4, :, :, core]
-    wc = remote(src, src, wc_s, wc_r, (sib, t))
-    wc.start()
     for cp in pcopies:
         cp.wait()
 
@@ -376,10 +388,16 @@
                 )
                 spread_ = jnp.mean(num * num, axis=-1, keepdims=True)
                 gh[half, d, :, h * DV : (h + 1) * DV] = (num * lax.rsqrt(spread_ + EPS)).astype(BF16)
-        if half == 0:
-            wocopy.wait()
-            wc.wait()
         for n, d in enumerate((1, 3, 2, 0)):
+            if half == 0:
+                if d:
+                    wc[d].wait()
+                else:
+                    wocopy.wait()
+            if half == 0 and n == 0:
+                wc[3] = across_cores(3)
+            if half == 0 and n == 1:
+                wc[2] = across_cores(2)
             acc = jnp.zeros((C, 512), F32)
             for p in range(TP):
                 acc = acc + jnp.dot(
@@ -443,11 +461,11 @@
             pltpu.VMEM((2, TP, C, VW), BF16),
             pltpu.VMEM((2, 4, C, 512), BF16),
             dma((3 + NC,)), dma((NC,)), dma, dma, dma, dma, dma, dma, dma, dma, dma,
-            dma((3,)), dma((3,)), dma((6,)), dma((6,)), dma((6,)), dma((6,)), dma, dma,
+            dma((3,)), dma((3,)), dma((6,)), dma((6,)), dma((18,)), dma((18,)), dma((3,)), dma((3,)),
             dma((2, 3)), dma((2, 3)), dma((3,)), dma((3,)), dma((2, 3)), dma((2, 3)), dma((2,)),
         ],
         compiler_params=pltpu.CompilerParams(
-            collective_id=0, has_side_effects=True, vmem_limit_bytes=50 * 1024 * 1024
+            collective_id=0, has_side_effects=True, vmem_limit_bytes=59 * 1024 * 1024
         ),
     )(
         tokens, gain, wt, conv_taps, w_out.reshape(4, 4, 2, 64, 512),

time: 93.7 us -> 83.3 us (0.89)
  Pallas kernels: 88.5 us -> 80 us
  local copies, waits for them, and re-layouts: 5.01 us -> 3.05 us
    pallas_call x1, Pallas kernels: 88.5 us -> 80 us  [body(): pl.pallas_call(kernel, out_shape=jax.ShapeDtypeStruct((T, 512), BF16), in...]
    unnamed x9 -> x1, local copies, waits for them, and re-layouts: 5.01 us -> 3.05 us
where the time goes in v4:
time: 83.3 us; the launch traced here: 83 us
  Pallas kernels  80 us (96%)
  local copies, waits for them, and re-layouts  3.05 us (4%)
    pallas_call x1, Pallas kernels, body(): pl.pallas_call(kernel, out_shape=jax.ShapeDtypeStruct((T, 512), BF16), in...  80 us
    unnamed x1, local copies, waits for them, and re-layouts  3.05 us

profile of v4, /device:TPU:1, one launch (start us, length us, event | category | flops | bytes accessed | tf_op | source)
XLA Modules:
  0.0 83.0 jit_solution(12509819488264563126)
XLA Ops:
  0.0 80.0 %shard_map.73 = bf16[2048,512]{1,0:T(8,128)(2,1)} custom-call(bf16[2048,2048]{1,0:T(8,128)(2,1)} %x_hbm.1, bf16[2048]{0:T(1024)(128)(2,1)} %gain_ref.1, bf16[640,2048]{1,0:T(8,128)(2,1)} %bitcast.4, bf16[3,4,160]{2,1,0:T(4,128)(2,1)} %taps_ref.1, bf16[4,4,2,64,512]{4,3,2,1,0:T(8,128)(2,1)} %bitcast.5, bf16[2,256,1024]{2,1,0:T(8,128)(2,1)} %constant.4.clone.eq_hbm, ...), custom_call_target="tpu_custom_call" | custom-call | tf_op jit(solution)/shard_map/pallas_call | solution.py:434
  80.0 3.0 %copy.9 = bf16[2048,512]{1,0:T(8,128)(2,1)} copy(bf16[2048,512]{1,0:T(8,128)(2,1)} %shard_map.73) | data formatting | bytes 4194304

commit v5 on v4

--- a/solution.py
+++ b/solution.py
@@ -61,7 +61,7 @@
     x_hbm, gain_ref, wt_hbm, taps_ref, wo_hbm, eq_hbm, ek_hbm,
     out_ref,
     xv, xt8, wv, wg, eqv, ekv, taps, pf, tl, mx, ga, sc, nl, fq, sb, r1, p2, r2, ps, pp, wf, gh, ob,
-    in_sem, x_sem, wo_sem, halo_s, halo_r, s1_s, s1_r, s2_s, s2_r, s3_s, s3_r,
+    in_sem, w_sem, x_sem, wo_sem, halo_s, halo_r, s1_s, s1_r, s2_s, s2_r, s3_s, s3_r,
     wx_s, wx_r, wa_s, wa_r, wb_s, wb_r, wc_s, wc_r, a_s, a_r, q_s, q_r, b_s, b_r, own_s,
 ):
     s = lax.axis_index("seq")
@@ -91,8 +91,12 @@
 
     tiles = [(d, half) for half in (1, 0) for d in (1, 3, 2)] + [(0, 1), (0, 0)]
 
-    wcopy = pltpu.make_async_copy(wt_hbm, wv, in_sem.at[0])
-    wcopy.start()
+    wcopies = []
+    for h in range(HL):
+        rows = pl.ds(160 * h, 160)
+        cp = pltpu.make_async_copy(wt_hbm.at[rows], wv.at[rows], w_sem.at[h])
+        cp.start()
+        wcopies.append(cp)
     tcopies = []
     for c in range(NC):
         cp = pltpu.make_async_copy(x_hbm.at[pl.ds(c * C + C - 8, 8)], xt8.at[pl.ds(8 * c, 8)], in_sem.at[3 + c])
@@ -136,9 +140,9 @@
             tq = tq + jnp.dot(tk, pick_q, preferred_element_type=F32)[h : h + 1, :]
         taps[k : k + 1, VW:] = tq
 
-    wcopy.wait()
     gain = gain_ref[...].astype(F32)[None, :]
     for h in range(HL):
+        wcopies[h].wait()
         for r in range(0, 160, 32):
             dst = VW + 32 * h if r == 0 else h * DV + r - 32
             src = h * 160 + r
@@ -348,7 +352,9 @@
         remote(sb.at[chip], r1.at[s], s3_s, s1_r, (s - 1, t)).wait_send()
         fwd.wait_recv()
 
-    pcopies = []
+    onward(3)
+
+    pcopies = {}
     for d in (1, 3, 2, 0):
         n = near(d)
         for k in range(CHIPS):
@@ -361,9 +367,8 @@
         if d:
             cp = remote(ps.at[d - 1], pp.at[t, :, 0:F, :], q_s.at[d - 1], q_r.at[d - 1], xpeer(d))
             cp.start()
-            pcopies.append(cp)
+            pcopies[d] = cp
     wc = {1: across_cores(1)}
-    onward(3)
     onward(2)
 
     for d in (3, 1, 2):
@@ -375,13 +380,13 @@
     def _():
         fwd.wait_send()
 
-    for cp in pcopies:
-        cp.wait()
 
     results = []
     own = []
     for half in range(2):
-        for d in range(TP):
+        for d in (0, 3, 1, 2):
+            if half == 0 and d:
+                pcopies[TP - d].wait_recv()
             for h in range(HL):
                 num = nl[half, d, :, h * DV : (h + 1) * DV] + jnp.dot(
                     fq[half, d, :, h * FP : (h + 1) * FP], pp[near(d), h], preferred_element_type=F32
@@ -414,7 +419,7 @@
                 cp.start()
                 own.append(cp)
 
-    for cp in sent + results:
+    for cp in sent + results + list(pcopies.values()):
         cp.wait_send()
     for half in range(2):
         for d in range(1, TP):
@@ -424,6 +429,17 @@
         cp.wait()
 
 
+def copy_kernel(src_ref, dst_ref, sem):
+    copies = []
+    for i in range(8):
+        rows = pl.ds(i * (T // 8), T // 8)
+        cp = pltpu.make_async_copy(src_ref.at[rows], dst_ref.at[rows], sem.at[i])
+        cp.start()
+        copies.append(cp)
+    for cp in copies:
+        cp.wait()
+
+
 def body(tokens, gain, w_in, conv_taps, w_out):
     wt = jnp.transpose(w_in, (1, 2, 0)).reshape(HL * 160, D)
     eq, ek = feature_maps()
@@ -431,7 +447,7 @@
     vmem = pl.BlockSpec(memory_space=pltpu.VMEM)
     dma = pltpu.SemaphoreType.DMA
     width = VW + QW
-    return pl.pallas_call(
+    result = pl.pallas_call(
         kernel,
         out_shape=jax.ShapeDtypeStruct((T, 512), BF16),
         in_specs=[hbm, vmem, hbm, vmem, hbm, hbm, hbm],
@@ -460,7 +476,7 @@
             pltpu.VMEM((4, 4, 4, 2, 64, 512), BF16),
             pltpu.VMEM((2, TP, C, VW), BF16),
             pltpu.VMEM((2, 4, C, 512), BF16),
-            dma((3 + NC,)), dma((NC,)), dma, dma, dma, dma, dma, dma, dma, dma, dma,
+            dma((3 + NC,)), dma((HL,)), dma((NC,)), dma, dma, dma, dma, dma, dma, dma, dma, dma,
             dma((3,)), dma((3,)), dma((6,)), dma((6,)), dma((18,)), dma((18,)), dma((3,)), dma((3,)),
             dma((2, 3)), dma((2, 3)), dma((3,)), dma((3,)), dma((2, 3)), dma((2, 3)), dma((2,)),
         ],
@@ -471,6 +487,13 @@
         tokens, gain, wt, conv_taps, w_out.reshape(4, 4, 2, 64, 512),
         jnp.asarray(eq), jnp.asarray(ek),
     )
+    return pl.pallas_call(
+        copy_kernel,
+        out_shape=jax.ShapeDtypeStruct((T, 512), BF16),
+        in_specs=[hbm],
+        out_specs=hbm,
+        scratch_shapes=[dma((8,))],
+    )(result)
 
 
 def solution(mesh):

time: 83.3 us -> 146 us (1.75)
  Pallas kernels: 80 us -> 146 us
  local copies, waits for them, and re-layouts: 3.05 us -> 0 us
    pallas_call x0 -> x1, Pallas kernels: none -> 64.7 us  [body(): pl.pallas_call(copy_kernel, out_shape=jax.ShapeDtypeStruct((T, 512), BF16...]
    unnamed x1 -> x0, local copies, waits for them, and re-layouts: 3.05 us -> none
where the time goes in v5:
time: 146 us
  Pallas kernels  146 us (100%)
    pallas_call x1, Pallas kernels, body(): pl.pallas_call(kernel, out_shape=jax.ShapeDtypeStruct((T, 512), BF16), in...  81 us
    pallas_call x1, Pallas kernels, body(): pl.pallas_call(copy_kernel, out_shape=jax.ShapeDtypeStruct((T, 512), BF16...  64.7 us

profile of v5, /device:TPU:1, one launch (start us, length us, event | category | flops | bytes accessed | tf_op | source)
XLA Modules:
  0.0 145.9 jit_solution(356337379010268580)
XLA Ops:
  0.0 81.0 %shard_map.73.src_ref = bf16[2048,512]{1,0:T(8,128)(2,1)} custom-call(bf16[2048,2048]{1,0:T(8,128)(2,1)} %x_hbm.1, bf16[2048]{0:T(1024)(128)(2,1)} %gain_ref.1, bf16[640,2048]{1,0:T(8,128)(2,1)} %bitcast.4, bf16[3,4,160]{2,1,0:T(4,128)(2,1)} %taps_ref.1, bf16[4,4,2,64,512]{4,3,2,1,0:T(8,128)(2,1)} %bitcast.5, bf16[2,256,1024]{2,1,0:T(8,128)(2,1)} %constant.4.clone.eq_hbm, ...), custom_call_target="tpu_custom_call" | custom-call | tf_op jit(solution)/shard_map/pallas_call | solution.py:450
  81.0 64.7 %shard_map.74 = bf16[2048,512]{1,0:T(8,128)(2,1)} custom-call(bf16[2048,512]{1,0:T(8,128)(2,1)} %shard_map.73.src_ref), custom_call_target="tpu_custom_call" | custom-call | tf_op jit(solution)/shard_map/pallas_call | solution.py:490

commit v6 on v4

--- a/solution.py
+++ b/solution.py
@@ -424,6 +424,21 @@
         cp.wait()
 
 
+def copy_kernel(src_ref, dst_ref, buf, in_sem, out_sem):
+    loads, stores = [], []
+    for i in range(8):
+        rows = pl.ds(i * (T // 8), T // 8)
+        loads.append(pltpu.make_async_copy(src_ref.at[rows], buf.at[rows], in_sem.at[i]))
+        stores.append(pltpu.make_async_copy(buf.at[rows], dst_ref.at[rows], out_sem.at[i]))
+    for cp in loads:
+        cp.start()
+    for load, store in zip(loads, stores):
+        load.wait()
+        store.start()
+    for cp in stores:
+        cp.wait()
+
+
 def body(tokens, gain, w_in, conv_taps, w_out):
     wt = jnp.transpose(w_in, (1, 2, 0)).reshape(HL * 160, D)
     eq, ek = feature_maps()
@@ -431,7 +446,7 @@
     vmem = pl.BlockSpec(memory_space=pltpu.VMEM)
     dma = pltpu.SemaphoreType.DMA
     width = VW + QW
-    return pl.pallas_call(
+    result = pl.pallas_call(
         kernel,
         out_shape=jax.ShapeDtypeStruct((T, 512), BF16),
         in_specs=[hbm, vmem, hbm, vmem, hbm, hbm, hbm],
@@ -471,6 +486,13 @@
         tokens, gain, wt, conv_taps, w_out.reshape(4, 4, 2, 64, 512),
         jnp.asarray(eq), jnp.asarray(ek),
     )
+    return pl.pallas_call(
+        copy_kernel,
+        out_shape=jax.ShapeDtypeStruct((T, 512), BF16),
+        in_specs=[hbm],
+        out_specs=hbm,
+        scratch_shapes=[pltpu.VMEM((T, 512), BF16), dma((8,)), dma((8,))],
+    )(result)
 
 
 def solution(mesh):

time: 83.3 us -> 82.8 us (level)
  local copies, waits for them, and re-layouts: 3.05 us -> 0 us
  Pallas kernels: 80 us -> 82.4 us
    unnamed x1 -> x0, local copies, waits for them, and re-layouts: 3.05 us -> none
    pallas_call x0 -> x1, Pallas kernels: none -> 2.39 us  [body(): pl.pallas_call(copy_kernel, out_shape=jax.ShapeDtypeStruct((T, 512), BF16...]
where the time goes in v6:
time: 82.8 us; the launch traced here: 82.5 us
  Pallas kernels  82.4 us (100%)
    pallas_call x1, Pallas kernels, body(): pl.pallas_call(kernel, out_shape=jax.ShapeDtypeStruct((T, 512), BF16), in...  80 us
    pallas_call x1, Pallas kernels, body(): pl.pallas_call(copy_kernel, out_shape=jax.ShapeDtypeStruct((T, 512), BF16...  2.39 us

profile of v6, /device:TPU:1, one launch (start us, length us, event | category | flops | bytes accessed | tf_op | source)
XLA Modules:
  0.0 82.5 jit_solution(10610219660776934756)
XLA Ops:
  0.0 80.0 %shard_map.73.src_ref = bf16[2048,512]{1,0:T(8,128)(2,1)} custom-call(bf16[2048,2048]{1,0:T(8,128)(2,1)} %x_hbm.1, bf16[2048]{0:T(1024)(128)(2,1)} %gain_ref.1, bf16[640,2048]{1,0:T(8,128)(2,1)} %bitcast.4, bf16[3,4,160]{2,1,0:T(4,128)(2,1)} %taps_ref.1, bf16[4,4,2,64,512]{4,3,2,1,0:T(8,128)(2,1)} %bitcast.5, bf16[2,256,1024]{2,1,0:T(8,128)(2,1)} %constant.4.clone.eq_hbm, ...), custom_call_target="tpu_custom_call" | custom-call | tf_op jit(solution)/shard_map/pallas_call | solution.py:449
  80.0 2.4 %shard_map.74 = bf16[2048,512]{1,0:T(8,128)(2,1)} custom-call(bf16[2048,512]{1,0:T(8,128)(2,1)} %shard_map.73.src_ref), custom_call_target="tpu_custom_call" | custom-call | tf_op jit(solution)/shard_map/pallas_call | solution.py:489

commit v7 on v6

--- a/solution.py
+++ b/solution.py
@@ -378,6 +378,7 @@
     for cp in pcopies:
         cp.wait()
 
+    wc[3] = across_cores(3)
     results = []
     own = []
     for half in range(2):
@@ -390,14 +391,12 @@
                 gh[half, d, :, h * DV : (h + 1) * DV] = (num * lax.rsqrt(spread_ + EPS)).astype(BF16)
         for n, d in enumerate((1, 3, 2, 0)):
             if half == 0:
+                if n == 1:
+                    wc[2] = across_cores(2)
                 if d:
                     wc[d].wait()
                 else:
                     wocopy.wait()
-            if half == 0 and n == 0:
-                wc[3] = across_cores(3)
-            if half == 0 and n == 1:
-                wc[2] = across_cores(2)
             acc = jnp.zeros((C, 512), F32)
             for p in range(TP):
                 acc = acc + jnp.dot(

time: 82.8 us -> 82.8 us (level)
  no operation moved by 1% of the time
where the time goes in v7:
time: 82.8 us; the launch traced here: 82.5 us
  Pallas kernels  82.4 us (100%)
    pallas_call x1, Pallas kernels, body(): pl.pallas_call(kernel, out_shape=jax.ShapeDtypeStruct((T, 512), BF16), in...  80 us
    pallas_call x1, Pallas kernels, body(): pl.pallas_call(copy_kernel, out_shape=jax.ShapeDtypeStruct((T, 512), BF16...  2.39 us

profile of v7, /device:TPU:1, one launch (start us, length us, event | category | flops | bytes accessed | tf_op | source)
XLA Modules:
  0.0 82.5 jit_solution(8317148064672934333)
XLA Ops:
  0.0 80.0 %shard_map.73.src_ref = bf16[2048,512]{1,0:T(8,128)(2,1)} custom-call(bf16[2048,2048]{1,0:T(8,128)(2,1)} %x_hbm.1, bf16[2048]{0:T(1024)(128)(2,1)} %gain_ref.1, bf16[640,2048]{1,0:T(8,128)(2,1)} %bitcast.4, bf16[3,4,160]{2,1,0:T(4,128)(2,1)} %taps_ref.1, bf16[4,4,2,64,512]{4,3,2,1,0:T(8,128)(2,1)} %bitcast.5, bf16[2,256,1024]{2,1,0:T(8,128)(2,1)} %constant.4.clone.eq_hbm, ...), custom_call_target="tpu_custom_call" | custom-call | tf_op jit(solution)/shard_map/pallas_call | solution.py:448
  80.0 2.4 %shard_map.74 = bf16[2048,512]{1,0:T(8,128)(2,1)} custom-call(bf16[2048,512]{1,0:T(8,128)(2,1)} %shard_map.73.src_ref), custom_call_target="tpu_custom_call" | custom-call | tf_op jit(solution)/shard_map/pallas_call | solution.py:488
